TPU v7x, 256 devices: a whole 4x4x8 slice. The times are simulated.
256 devices in a mesh: grp: 8 (over z), tp: 32 (over y, x, core).
Axes of the slice: x: 4, y: 4, z: 8, core: 2. Of those that a mesh axis runs over, the one named last changes fastest.
Arguments:
- hidden_in: bfloat16 [512, 4096], P('grp'), may hold values from -6 to 6
- norm_gain: float32 [4096], replicated, may hold values from 0.25 to 1.75
- head_weight: bfloat16 [4096, 128256], P('grp', 'tp'), may hold values from -1 to 1
- ffn_act: bfloat16 [512, 14336], P('grp', 'tp'), may hold values from -6 to 6
- labels: int32 [512], P('grp'), may hold values from 0 to 128255
- lengths: int32 [64], P('grp'), may hold values from 1 to 8
- proj_hidden: bfloat16 [4096, 64], replicated, may hold values from -0.09375 to 0.09375
- proj_vocab: bfloat16 [128256, 64], P('tp'), may hold values from -6 to 6
- proj_ffn: bfloat16 [14336, 64], P('tp'), may hold values from -0.046875 to 0.046875
- proj_down: bfloat16 [4096, 64], replicated, may hold values from -6 to 6
- store: bfloat16 [65536, 8192], P('grp', 'tp'), may hold values from -0.0625 to 0.0625
Outputs:
- scores: float32 [64, 65536], P('tp', 'grp')
All inputs are finite; a program needn't handle non-finite values.
Results may differ from a plain program's by a relative error of at most 0.012.
Values may be sent and summed in bfloat16 or wider, within the bound.
No kernel may reach another device: no remote copies, remote signals or barrier semaphores. Data moves between devices by JAX's collectives and lax.ppermute only.
A program may use at most 64 MiB of HBM per device.

v0:
```python
import jax
import jax.numpy as jnp
from jax import lax
from jax.sharding import PartitionSpec as P

epsilon = 1e-05
highest = lax.Precision.HIGHEST


def sent_to_all(value, axis):
    copies = jnp.broadcast_to(value, (lax.axis_size(axis), *value.shape))
    return lax.all_to_all(copies, axis, split_axis=0, concat_axis=0, tiled=True)


def over_copies(value, axis):
    everything = sent_to_all(value, axis)
    return jnp.max(everything, axis=0)


def of_everyone(value, axis):
    everything = sent_to_all(value, axis)
    return jnp.sum(everything, axis=0)


def packed_total(arrays, axis):
    vector, at, outs = (jnp.concatenate([a.reshape(-1) for a in arrays]), 0, [])
    so_far = of_everyone(vector, axis)
    for a in arrays:
        outs.append(so_far[at : at + a.size].reshape(a.shape))
        at += a.size
    return tuple(outs)


def laid_out(tiles, dim):
    shape = list(tiles.shape[1:])
    shape[dim] *= tiles.shape[0]
    return jnp.moveaxis(tiles, 0, dim).reshape(shape)


def gather_directly(value, axis, dim):
    tiles = sent_to_all(value, axis)
    return laid_out(tiles, dim)


def cut_along(value, dim, length):
    before, after = (value.shape[:dim], value.shape[dim + 1 :])
    return jnp.moveaxis(value.reshape(*before, length, -1, *after), dim, 0)


def sent_and_summed(value, axis, dim):
    tiles = cut_along(value, dim, lax.axis_size(axis))
    arrived = lax.all_to_all(tiles, axis, split_axis=0, concat_axis=0, tiled=True)
    return arrived.sum(axis=0)


def fold_rows(pieces, high_part, low_part):
    contract = (((0,), (0,)), ((), ()))
    upper = lax.dot_general(pieces, high_part, contract, preferred_element_type=jnp.float32)
    return upper + lax.dot_general(pieces, low_part, contract, preferred_element_type=jnp.float32)


def per_device(
    hidden_in,
    norm_gain,
    head_weight,
    ffn_act,
    labels,
    lengths,
    proj_hidden,
    proj_vocab,
    proj_ffn,
    proj_down,
    store,
):
    token_count, model_width = hidden_in.shape
    query_here = lengths.shape[0]
    seq_span = token_count // query_here
    rows_owned, vocab_owned = head_weight.shape
    rank_size = proj_hidden.shape[1]
    group_index = lax.axis_index("grp")
    vocab_index = lax.axis_index("tp")
    wide_hidden = hidden_in.astype(jnp.float32)
    inverse = lax.rsqrt(jnp.mean(wide_hidden * wide_hidden, axis=1, keepdims=True) + epsilon)
    unit_hidden = wide_hidden * inverse
    normed = (norm_gain * unit_hidden).astype(jnp.bfloat16)
    gained_down = norm_gain[:, None] * proj_down.astype(jnp.float32)
    down_high = gained_down.astype(jnp.bfloat16)
    down_low = (gained_down - down_high.astype(jnp.float32)).astype(jnp.bfloat16)
    spread = lax.all_to_all(normed, "grp", split_axis=1, concat_axis=0, tiled=True)
    logits = lax.psum_scatter(
        jnp.dot(spread, head_weight, preferred_element_type=jnp.float32),
        "grp",
        scatter_dimension=0,
        tiled=True,
    )
    local_max = jnp.max(logits, axis=1)
    peak = over_copies(local_max, "tp")
    denominator = of_everyone(jnp.sum(jnp.exp(logits - peak[:, None]), axis=1), "tp")
    probs = jnp.exp(logits - peak[:, None]) / denominator[:, None]
    positions = lax.broadcasted_iota(jnp.int32, (token_count,), 0) % seq_span
    valid = positions < jnp.repeat(lengths, seq_span)
    vocab_ids = vocab_index * vocab_owned + lax.broadcasted_iota(jnp.int32, (1, vocab_owned), 1)
    onehot = (labels[:, None] == vocab_ids).astype(jnp.float32)
    grads = jnp.where(valid[:, None], probs - onehot, 0.0).astype(jnp.bfloat16)
    own_high = lax.dynamic_slice_in_dim(down_high, group_index * rows_owned, rows_owned, 0)
    own_low = lax.dynamic_slice_in_dim(down_low, group_index * rows_owned, rows_owned, 0)
    local_fold = fold_rows(head_weight, own_high, own_low)
    folded_sum = lax.psum(local_fold, "grp")
    down_sum = jnp.dot(grads.astype(jnp.float32), folded_sum, precision=highest)
    head_side = jnp.dot(grads, proj_vocab, preferred_element_type=jnp.float32)
    label_dot = jnp.sum(grads.astype(jnp.float32) * logits, axis=1)
    ffn_side = jnp.dot(ffn_act, proj_ffn, preferred_element_type=jnp.float32)
    head_side, down_sum, label_dot, ffn_side = packed_total(
        (head_side, down_sum, label_dot, ffn_side), "tp"
    )
    hidden_side = jnp.dot(normed, proj_hidden, preferred_element_type=jnp.float32)
    unit_down = jnp.dot(unit_hidden, proj_down.astype(jnp.float32), precision=highest)
    down_side = inverse * (down_sum - (label_dot / model_width)[:, None] * unit_down)
    shaped = (query_here, seq_span, rank_size)
    first_outer = jnp.einsum("spa,spb->sab", hidden_side.reshape(shaped), head_side.reshape(shaped))
    second_outer = jnp.einsum("spa,spb->sab", ffn_side.reshape(shaped), down_side.reshape(shaped))
    queries = jnp.concatenate(
        [first_outer.reshape(query_here, -1), second_outer.reshape(query_here, -1)], axis=1
    ).astype(jnp.bfloat16)
    feature_owned = store.shape[1]
    own_queries = lax.dynamic_slice_in_dim(queries, vocab_index * feature_owned, feature_owned, 1)
    every_query = gather_directly(own_queries, "grp", 0)
    return sent_and_summed(
        lax.dot_general(
            every_query, store, (((1,), (1,)), ((), ())), preferred_element_type=jnp.float32
        ),
        "tp",
        0,
    )


def solution(mesh):
    return jax.shard_map(
        per_device,
        mesh=mesh,
        in_specs=(
            P("grp", None),
            P(),
            P("grp", "tp"),
            P("grp", "tp"),
            P("grp"),
            P("grp"),
            P(),
            P("tp", None),
            P("tp", None),
            P(),
            P("grp", "tp"),
        ),
        out_specs=P("tp", "grp"),
        check_vma=False,
    )
```

profile of v0, /device:TPU:1, one launch (start us, length us, event | category | flops | bytes accessed | tf_op | source)
XLA Modules:
  0.0 308.6 jit_solution(2016261024021584329)
XLA Ops:
  6.5 0.0 copy-start
  6.5 0.0 reduce-scatter.2.cloned.1.call-start
  6.5 1.3 fusion.10
  7.9 1.2 fusion.9
  9.1 24.9 %all_to_all.47 = bf16[64,8,512]{2,0,1:T(8,128)(2,1)S(1)} all-to-all(bf16[64,8,512]{2,0,1:T(8,128)(2,1)S(1)} %bitcast.38), channel_id=1, replica_groups=mesh['grp'=8,'tp'=32] {'grp'}, dimensions={1} | all-to-all | bytes 1048576 | tf_op jit(solution)/shard_map/all_to_all | solution.py:89
  34.1 7.8 %fusion.25 = f32[512,4008]{1,0:T(8,128)} fusion(bf16[512,512]{1,0:T(8,128)(2,1)S(1)} %bitcast.37, bf16[512,4008]{0,1:T(8,128)(2,1)} %param.13), kind=kOutput, calls=%fused_computation.42 | convolution fusion | flops 2101346304 | bytes 12836864 | tf_op jit(solution)/shard_map/dot_general | solution.py:91
  41.9 0.0 reduce-scatter.2.cloned.1.call-update
  41.9 0.0 all-reduce.2.cloned.1.call-start
  42.0 1.0 copy-done.3
  42.9 0.0 copy-done.5
  42.9 0.1 convert_multiply_fusion.11
  43.1 3.7 %fusion.17 = f32[64,4008]{1,0:T(8,128)S(1)} fusion(bf16[512,4008]{0,1:T(8,128)(2,1)} %param.13, bf16[4096,64]{0,1:T(8,128)(2,1)S(1)} %get-tuple-element.8, s32[]{:T(128)S(6)} %select_n.24), kind=kOutput, calls=%fused_computation.30 | convolution fusion | flops 262668288 | bytes 5195780 | tf_op jit(solution)/shard_map/dot_general | solution.py:58
  46.7 0.0 copy-start.9
  46.7 0.0 copy-start.6
  46.8 0.0 copy-start.7
  46.8 0.0 copy-done.1
  46.8 0.0 copy-start.8
  46.8 2.3 fusion
  49.1 0.0 all-reduce.2.cloned.1.call-update
  49.2 0.0 copy-done.9
  49.2 0.1 broadcast_in_dim.36
  49.2 0.1 reshape.90
  49.3 0.0 copy-done.6
  49.3 0.0 copy-done.7
  49.3 0.2 fusion.28
  49.5 85.5 %reduce-scatter.2.cloned.1.call-done = f32[64,4008]{1,0:T(8,128)} async-done(((f32[512,4008]{1,0:T(8,128)}), f32[64,4008]{1,0:T(8,128)}) %reduce-scatter.2.cloned.1.call-update) | async-done | bytes 1026064 | tf_op jit(solution)/shard_map/reduce_scatter | solution.py:90
  134.9 1.4 reduce_max.18
  136.3 0.6 broadcast_in_dim.38
  136.9 7.6 %all-to-all-start.1 = ((f32[32,1,64]{2,1,0:T(1,128)}), f32[32,1,64]{2,1,0:T(1,128)S(1)}, u32[]{:S(2)}, u32[]{:S(2)}) async-start(f32[32,1,64]{2,1,0:T(1,128)} %broadcast_in_dim.38), calls=%async_computation.2 | async-start | bytes 32768 | tf_op jit(solution)/shard_map/all_to_all | solution.py:12
  144.5 6.9 %all-to-all-done.1 = f32[32,1,64]{2,1,0:T(1,128)S(1)} async-done(((f32[32,1,64]{2,1,0:T(1,128)}), f32[32,1,64]{2,1,0:T(1,128)S(1)}, u32[]{:S(2)}, u32[]{:S(2)}) %all-to-all-start.1) | async-done | bytes 8224 | tf_op jit(solution)/shard_map/all_to_all | solution.py:12
  151.4 1.5 fusion.11
  153.0 0.6 broadcast_in_dim.39
  153.6 4.1 %all-to-all-start.2 = ((f32[32,1,64]{2,1,0:T(1,128)}), f32[32,1,64]{2,1,0:T(1,128)S(1)}, u32[]{:S(2)}, u32[]{:S(2)}) async-start(f32[32,1,64]{2,1,0:T(1,128)} %broadcast_in_dim.39), calls=%async_computation.3 | async-start | bytes 32768 | tf_op jit(solution)/shard_map/all_to_all | solution.py:12
  157.8 0.1 reshape.93
  157.8 6.9 %all-to-all-done.2 = f32[32,1,64]{2,1,0:T(1,128)S(1)} async-done(((f32[32,1,64]{2,1,0:T(1,128)}), f32[32,1,64]{2,1,0:T(1,128)S(1)}, u32[]{:S(2)}, u32[]{:S(2)}) %all-to-all-start.2) | async-done | bytes 8224 | tf_op jit(solution)/shard_map/all_to_all | solution.py:12
  164.8 0.0 copy-done.8
  164.8 1.8 multiply_reduce_fusion
  166.6 0.0 copy-done.4
  166.6 0.3 fusion.26
  166.9 0.1 reshape.91
  166.9 40.7 %all-reduce.2.cloned.1.call-done = f32[4008,64]{0,1:T(8,128)} async-done(((f32[4008,64]{0,1:T(8,128)}), f32[4008,64]{0,1:T(8,128)}) %all-reduce.2.cloned.1.call-update) | async-done | bytes 1026064 | tf_op jit(solution)/shard_map/psum | solution.py:108
  207.6 1.9 fusion.27
  209.5 0.0 copy-start.2
  209.5 0.1 reshape.92
  209.6 0.1 concatenate.7
  209.7 2.0 broadcast_in_dim.41
  211.6 11.9 %all-to-all-start.3 = ((f32[32,1,12352]{2,1,0:T(1,128)}), f32[32,1,12352]{2,1,0:T(1,128)S(1)}, u32[]{:S(2)}, u32[]{:S(2)}) async-start(f32[32,1,12352]{2,1,0:T(1,128)} %broadcast_in_dim.41), calls=%async_computation.4 | async-start | bytes 3178496 | tf_op jit(solution)/shard_map/all_to_all | solution.py:12
  223.6 22.4 %all-to-all-done.3 = f32[32,1,12352]{2,1,0:T(1,128)S(1)} async-done(((f32[32,1,12352]{2,1,0:T(1,128)}), f32[32,1,12352]{2,1,0:T(1,128)S(1)}, u32[]{:S(2)}, u32[]{:S(2)}) %all-to-all-start.3) | async-done | bytes 1581088 | tf_op jit(solution)/shard_map/all_to_all | solution.py:12
  246.0 0.9 reduce_sum.58
  246.9 0.1 fusion.24
  247.0 0.1 reshape_reshape.6
  247.1 0.0 copy-done
  247.1 0.6 convolution_convert_fusion.1
  247.7 0.2 reshape.94
  247.9 0.1 reshape_reshape.7
  248.0 0.1 reshape.95
  248.0 1.8 fusion.8
  249.8 0.2 fusion.29
  250.0 0.2 reshape.97
  250.3 10.6 %all_to_all.48 = bf16[8,8,256]{2,1,0:T(8,128)(2,1)S(1)} all-to-all(bf16[8,8,256]{2,1,0:T(8,128)(2,1)S(1)} %broadcast_in_dim.42), channel_id=1, replica_groups=mesh['grp'=8,'tp'=32] {'grp'}, dimensions={0} | all-to-all | bytes 65536 | tf_op jit(solution)/shard_map/all_to_all | solution.py:12
  260.8 3.6 %fusion.1 = f32[32,2,8192]{2,0,1:T(8,128)S(1)} fusion(bf16[8192,256]{1,0:T(8,128)(2,1)} %param.21, bf16[32,2,256]{2,1,0:T(2,128)(2,1)S(1)} %dot_general.45), kind=kOutput, calls=%fused_computation.2 | convolution fusion | flops 268435456 | bytes 6324224 | tf_op jit(solution)/shard_map/dot_general | solution.py:129
  264.4 1.6 copy.26
  266.0 34.4 %all_to_all.49 = f32[32,2,8192]{2,1,0:T(2,128)S(1)} all-to-all(f32[32,2,8192]{2,1,0:T(2,128)S(1)} %copy.26), channel_id=1, replica_groups=mesh['grp'=8,'tp'=32] {'tp'}, dimensions={0} | all-to-all | bytes 4194304 | tf_op jit(solution)/shard_map/all_to_all | solution.py:52
  300.4 1.4 reduce_sum.59
  (16 shorter events, 0.2 us)
Async XLA Ops:
  6.5 240.6 %copy-start = (bf16[4096,64]{0,1:T(8,128)(2,1)S(1)}, bf16[4096,64]{0,1:T(8,128)(2,1)}, u32[]{:S(2)}) copy-start(bf16[4096,64]{0,1:T(8,128)(2,1)} %param.17) | copy-start | bytes 1572868
  6.5 128.4 %reduce-scatter.2.cloned.1.call-start = ((), (), s32[]{:S(2)}) async-start(), calls=%async_computation.7 | async-start | bytes 9437184 | tf_op jit(solution)/shard_map/reduce_scatter | solution.py:90
  41.9 1.0 copy-start.3
  41.9 1.0 copy-start.5
  41.9 165.7 %all-reduce.2.cloned.1.call-start = ((), (), s32[]{:S(2)}) async-start(), calls=%async_computation.8 | async-start | bytes 2097152 | tf_op jit(solution)/shard_map/psum | solution.py:108
  42.9 3.9 %copy-start.1 = (bf16[512,4008]{0,1:T(8,128)(2,1)S(1)}, bf16[512,4008]{0,1:T(8,128)(2,1)}, u32[]{:S(2)}) copy-start(bf16[512,4008]{0,1:T(8,128)(2,1)} %param.13) | copy-start | bytes 12312580
  46.7 2.4 copy-start.9
  46.7 2.6 copy-start.6
  46.8 2.6 copy-start.7
  46.8 118.0 %copy-start.8 = (s32[64]{0:T(128)S(1)}, s32[64]{0:T(128)}, u32[]{:S(2)}) copy-start(s32[64]{0:T(128)} %param.15) | copy-start | bytes 772
  49.1 117.4 %copy-start.4 = (bf16[4008,64]{0,1:T(8,128)(2,1)S(1)}, bf16[4008,64]{0,1:T(8,128)(2,1)}, u32[]{:S(2)}) copy-start(bf16[4008,64]{0,1:T(8,128)(2,1)} %param.18) | copy-start | bytes 1539076
  136.9 14.5 %all-to-all-start.1 = ((f32[32,1,64]{2,1,0:T(1,128)}), f32[32,1,64]{2,1,0:T(1,128)S(1)}, u32[]{:S(2)}, u32[]{:S(2)}) async-start(f32[32,1,64]{2,1,0:T(1,128)} %broadcast_in_dim.38), calls=%async_computation.2 | async-start | bytes 32768 | tf_op jit(solution)/shard_map/all_to_all | solution.py:12
  153.6 11.1 %all-to-all-start.2 = ((f32[32,1,64]{2,1,0:T(1,128)}), f32[32,1,64]{2,1,0:T(1,128)S(1)}, u32[]{:S(2)}, u32[]{:S(2)}) async-start(f32[32,1,64]{2,1,0:T(1,128)} %broadcast_in_dim.39), calls=%async_computation.3 | async-start | bytes 32768 | tf_op jit(solution)/shard_map/all_to_all | solution.py:12
  209.5 38.5 %copy-start.2 = (bf16[64,4096]{1,0:T(8,128)(2,1)S(1)}, bf16[64,4096]{1,0:T(8,128)(2,1)}, u32[]{:S(2)}) copy-start(bf16[64,4096]{1,0:T(8,128)(2,1)} %param.11) | copy-start | bytes 1572868
  211.6 34.4 %all-to-all-start.3 = ((f32[32,1,12352]{2,1,0:T(1,128)}), f32[32,1,12352]{2,1,0:T(1,128)S(1)}, u32[]{:S(2)}, u32[]{:S(2)}) async-start(f32[32,1,12352]{2,1,0:T(1,128)} %broadcast_in_dim.41), calls=%async_computation.4 | async-start | bytes 3178496 | tf_op jit(solution)/shard_map/all_to_all | solution.py:12
Sparse Core Ops, SparseCore 0:
  42.0 92.8 reduce-scatter.1
  137.3 70.2 all-reduce.1
where the time goes:
time: 309 us
  waiting for transfers between devices  162 us (52%)
  blocking collectives  69.8 us (23%)
  starting transfers between devices  23.7 us (8%)
  matrix products  22.3 us (7%)
  between operations  13.7 us (4%)
  other arithmetic  9.72 us (3%)
  local copies, waits for them, and re-layouts  7.04 us (2%)
    reduce_scatter x1, waiting for transfers between devices, per_device(): lax.psum_scatter(jnp.dot(spread, head_weight, preferred_element_type=jnp....  85.5 us
    psum x1, waiting for transfers between devices, per_device(): folded_sum = lax.psum(local_fold, 'grp')  40.7 us
    all_to_all x3, waiting for transfers between devices, sent_to_all(): return lax.all_to_all(copies, axis, split_axis=0, concat_axis=0, tiled=True)  36.2 us
    all_to_all x1, blocking collectives, sent_and_summed(): lax.all_to_all(tiles, axis, split_axis=0, concat_axis=0, tiled=True)  34.4 us
    all_to_all x1, blocking collectives, per_device(): lax.all_to_all(normed, 'grp', split_axis=1, concat_axis=0, tiled=True)  24.9 us
    all_to_all x3, starting transfers between devices, sent_to_all(): return lax.all_to_all(copies, axis, split_axis=0, concat_axis=0, tiled=True)  23.6 us
    all_to_all x1, blocking collectives, sent_to_all(): return lax.all_to_all(copies, axis, split_axis=0, concat_axis=0, tiled=True)  10.6 us
    dot_general x1, matrix products, per_device(): jnp.dot(spread, head_weight, preferred_element_type=jnp.float32)  7.81 us
  transfers between devices with their start and end apart: 5, of which 5 were waited for; matrix products, arithmetic and copies ran while one was open for 4% of the time, Pallas kernels for 0%

commit v1 on v0

--- a/solution.py
+++ b/solution.py
@@ -105,7 +105,7 @@
     own_high = lax.dynamic_slice_in_dim(down_high, group_index * rows_owned, rows_owned, 0)
     own_low = lax.dynamic_slice_in_dim(down_low, group_index * rows_owned, rows_owned, 0)
     local_fold = fold_rows(head_weight, own_high, own_low)
-    folded_sum = lax.psum(local_fold, "grp")
+    folded_sum = jnp.sum(lax.all_gather(local_fold, "grp"), axis=0)
     down_sum = jnp.dot(grads.astype(jnp.float32), folded_sum, precision=highest)
     head_side = jnp.dot(grads, proj_vocab, preferred_element_type=jnp.float32)
     label_dot = jnp.sum(grads.astype(jnp.float32) * logits, axis=1)

time: 309 us -> 333 us (1.078)
  waiting for transfers between devices: 162 us -> 186 us
  starting transfers between devices: 23.7 us -> 19.5 us
  other arithmetic: 9.72 us -> 13.5 us
    all_gather x0 -> x1, waiting for transfers between devices: none -> 71.5 us  [per_device(): folded_sum = jnp.sum(lax.all_gather(local_fold, 'grp'), axis=0)]
    psum x1 -> x0, waiting for transfers between devices: 40.7 us -> none  [per_device(): folded_sum = lax.psum(local_fold, 'grp')]
    all_to_all x3, waiting for transfers between devices: 36.2 us -> 29.3 us  [sent_to_all(): return lax.all_to_all(copies, axis, split_axis=0, concat_axis=0, tiled=True)]
    reduce_sum x0 -> x1, other arithmetic: none -> 5.04 us  [per_device(): folded_sum = jnp.sum(lax.all_gather(local_fold, 'grp'), axis=0)]
    all_to_all x3, starting transfers between devices: 23.6 us -> 19.4 us  [sent_to_all(): return lax.all_to_all(copies, axis, split_axis=0, concat_axis=0, tiled=True)]
  transfers between devices with their start and end apart: 5 -> 5, of which waited for: 5 -> 4; matrix products, arithmetic and copies ran while one was open for 4% -> 5% of each run, Pallas kernels for 0% -> 0%
where the time goes in v1:
time: 333 us; the launch traced here: 332 us
  waiting for transfers between devices  186 us (56%)
  blocking collectives  70 us (21%)
  matrix products  22.3 us (7%)
  starting transfers between devices  19.5 us (6%)
  between operations  13.7 us (4%)
  other arithmetic  13.5 us (4%)
  local copies, waits for them, and re-layouts  7.04 us (2%)
    reduce_scatter x1, waiting for transfers between devices, per_device(): lax.psum_scatter(jnp.dot(spread, head_weight, preferred_element_type=jnp....  85.4 us
    all_gather x1, waiting for transfers between devices, per_device(): folded_sum = jnp.sum(lax.all_gather(local_fold, 'grp'), axis=0)  71.5 us
    all_to_all x1, blocking collectives, sent_and_summed(): lax.all_to_all(tiles, axis, split_axis=0, concat_axis=0, tiled=True)  34.4 us
    all_to_all x3, waiting for transfers between devices, sent_to_all(): return lax.all_to_all(copies, axis, split_axis=0, concat_axis=0, tiled=True)  29.3 us
    all_to_all x1, blocking collectives, per_device(): lax.all_to_all(normed, 'grp', split_axis=1, concat_axis=0, tiled=True)  24.9 us
    all_to_all x3, starting transfers between devices, sent_to_all(): return lax.all_to_all(copies, axis, split_axis=0, concat_axis=0, tiled=True)  19.4 us
    all_to_all x1, blocking collectives, sent_to_all(): return lax.all_to_all(copies, axis, split_axis=0, concat_axis=0, tiled=True)  10.7 us
    dot_general x1, matrix products, per_device(): jnp.dot(spread, head_weight, preferred_element_type=jnp.float32)  7.8 us
  transfers between devices with their start and end apart: 5, of which 4 were waited for; matrix products, arithmetic and copies ran while one was open for 5% of the time, Pallas kernels for 0%

profile of v1, /device:TPU:1, one launch (start us, length us, event | category | flops | bytes accessed | tf_op | source)
XLA Modules:
  0.0 332.3 jit_solution(9030924463216319571)
XLA Ops:
  6.5 0.0 copy-start
  6.5 0.0 reduce-scatter.2.cloned.1.call-start
  6.5 1.3 fusion.10
  7.9 1.2 fusion.9
  9.1 24.9 %all_to_all.47 = bf16[64,8,512]{2,0,1:T(8,128)(2,1)S(1)} all-to-all(bf16[64,8,512]{2,0,1:T(8,128)(2,1)S(1)} %bitcast.40), channel_id=1, replica_groups=mesh['grp'=8,'tp'=32] {'grp'}, dimensions={1} | all-to-all | bytes 1048576 | tf_op jit(solution)/shard_map/all_to_all | solution.py:89
  34.1 7.8 %fusion.25 = f32[512,4008]{1,0:T(8,128)} fusion(bf16[512,512]{1,0:T(8,128)(2,1)S(1)} %bitcast.39, bf16[512,4008]{0,1:T(8,128)(2,1)} %param.13), kind=kOutput, calls=%fused_computation.42 | convolution fusion | flops 2101346304 | bytes 12836864 | tf_op jit(solution)/shard_map/dot_general | solution.py:91
  41.9 0.0 reduce-scatter.2.cloned.1.call-update
  41.9 0.0 all-gather.4.cloned.1.call-start
  41.9 1.0 copy-done.4
  42.9 0.0 copy-done.6
  42.9 0.1 convert_multiply_fusion.11
  43.0 3.7 %fusion.17 = f32[64,4008]{1,0:T(8,128)S(1)} fusion(bf16[512,4008]{0,1:T(8,128)(2,1)} %param.13, bf16[4096,64]{0,1:T(8,128)(2,1)S(1)} %get-tuple-element.8, s32[]{:T(128)S(6)} %select_n.24), kind=kOutput, calls=%fused_computation.30 | convolution fusion | flops 262668288 | bytes 5195780 | tf_op jit(solution)/shard_map/dot_general | solution.py:58
  46.7 0.0 copy-start.10
  46.7 0.0 copy-start.7
  46.7 0.0 copy-start.8
  46.8 0.0 copy-done.1
  46.8 2.4 fusion
  49.2 0.0 all-gather.4.cloned.1.call-update
  49.2 0.0 copy-done.10
  49.2 0.1 broadcast_in_dim.36
  49.3 0.1 reshape.90
  49.4 0.0 copy-done.7
  49.4 0.0 copy-done.8
  49.4 0.2 fusion.28
  49.5 85.4 %reduce-scatter.2.cloned.1.call-done = f32[64,4008]{1,0:T(8,128)} async-done(((f32[512,4008]{1,0:T(8,128)}), f32[64,4008]{1,0:T(8,128)}) %reduce-scatter.2.cloned.1.call-update) | async-done | bytes 1026064 | tf_op jit(solution)/shard_map/reduce_scatter | solution.py:90
  134.9 1.4 reduce_max.18
  136.3 0.6 broadcast_in_dim.38
  136.9 7.6 %all-to-all-start.1 = ((f32[32,1,64]{2,1,0:T(1,128)}), f32[32,1,64]{2,1,0:T(1,128)S(1)}, u32[]{:S(2)}, u32[]{:S(2)}) async-start(f32[32,1,64]{2,1,0:T(1,128)} %broadcast_in_dim.38), calls=%async_computation.2 | async-start | bytes 32768 | tf_op jit(solution)/shard_map/all_to_all | solution.py:12
  144.5 6.9 %all-to-all-done.1 = f32[32,1,64]{2,1,0:T(1,128)S(1)} async-done(((f32[32,1,64]{2,1,0:T(1,128)}), f32[32,1,64]{2,1,0:T(1,128)S(1)}, u32[]{:S(2)}, u32[]{:S(2)}) %all-to-all-start.1) | async-done | bytes 8224 | tf_op jit(solution)/shard_map/all_to_all | solution.py:12
  151.4 1.5 fusion.11
  153.0 0.6 broadcast_in_dim.39
  153.6 4.1 %all-to-all-start.2 = ((f32[32,1,64]{2,1,0:T(1,128)}), f32[32,1,64]{2,1,0:T(1,128)S(1)}, u32[]{:S(2)}, u32[]{:S(2)}) async-start(f32[32,1,64]{2,1,0:T(1,128)} %broadcast_in_dim.39), calls=%async_computation.3 | async-start | bytes 32768 | tf_op jit(solution)/shard_map/all_to_all | solution.py:12
  157.8 0.1 reshape.93
  157.8 71.5 %all-gather.4.cloned.1.call-done = f32[8,4008,64]{1,2,0:T(8,128)} async-done(((f32[1,4008,64]{1,2,0:T(8,128)}), f32[8,4008,64]{1,2,0:T(8,128)}) %all-gather.4.cloned.1.call-update) | async-done | bytes 8208400 | tf_op jit(solution)/shard_map/all_gather | solution.py:108
  229.3 5.0 %reduce_sum.66 = f32[4008,64]{0,1:T(8,128)} reduce(f32[8,4008,64]{1,2,0:T(8,128)} %all-gather.4.cloned.1.call-done, f32[]{:T(128)} %constant.15.clone.1), dimensions={0}, to_apply=%region_6.7 | reduce | flops 1795584 | bytes 9234436 | tf_op jit(solution)/shard_map/reduce_sum | solution.py:108
  234.4 0.0 all-to-all-done.2
  234.4 0.0 copy-done.2
  234.4 0.5 multiply_reduce_fusion
  234.9 0.0 copy-done.5
  235.0 0.3 fusion.26
  235.3 0.1 reshape.91
  235.3 1.9 fusion.27
  237.2 0.0 copy-start.3
  237.2 0.1 reshape.92
  237.3 0.1 concatenate.7
  237.4 2.0 broadcast_in_dim.41
  239.3 7.7 %all-to-all-start.3 = ((f32[32,1,12352]{2,1,0:T(1,128)}), f32[32,1,12352]{2,1,0:T(1,128)S(1)}, u32[]{:S(2)}, u32[]{:S(2)}) async-start(f32[32,1,12352]{2,1,0:T(1,128)} %broadcast_in_dim.41), calls=%async_computation.4 | async-start | bytes 3178496 | tf_op jit(solution)/shard_map/all_to_all | solution.py:12
  247.1 22.4 %all-to-all-done.3 = f32[32,1,12352]{2,1,0:T(1,128)S(1)} async-done(((f32[32,1,12352]{2,1,0:T(1,128)}), f32[32,1,12352]{2,1,0:T(1,128)S(1)}, u32[]{:S(2)}, u32[]{:S(2)}) %all-to-all-start.3) | async-done | bytes 1581088 | tf_op jit(solution)/shard_map/all_to_all | solution.py:12
  269.5 0.9 reduce_sum.68
  270.4 0.1 fusion.24
  270.5 0.1 reshape_reshape.6
  270.6 0.6 convolution_convert_fusion.1
  271.2 0.2 reshape.94
  271.4 0.1 reshape_reshape.7
  271.4 0.1 reshape.95
  271.5 0.0 copy-done.3
  271.5 1.8 fusion.8
  273.3 0.2 fusion.29
  273.5 0.2 reshape.97
  273.8 10.7 %all_to_all.48 = bf16[8,8,256]{2,1,0:T(8,128)(2,1)S(1)} all-to-all(bf16[8,8,256]{2,1,0:T(8,128)(2,1)S(1)} %broadcast_in_dim.42), channel_id=1, replica_groups=mesh['grp'=8,'tp'=32] {'grp'}, dimensions={0} | all-to-all | bytes 65536 | tf_op jit(solution)/shard_map/all_to_all | solution.py:12
  284.5 3.6 %fusion.1 = f32[32,2,8192]{2,0,1:T(8,128)S(1)} fusion(bf16[8192,256]{1,0:T(8,128)(2,1)} %param.21, bf16[32,2,256]{2,1,0:T(2,128)(2,1)S(1)} %dot_general.45), kind=kOutput, calls=%fused_computation.2 | convolution fusion | flops 268435456 | bytes 6324224 | tf_op jit(solution)/shard_map/dot_general | solution.py:129
  288.0 1.6 copy.26
  289.7 34.4 %all_to_all.49 = f32[32,2,8192]{2,1,0:T(2,128)S(1)} all-to-all(f32[32,2,8192]{2,1,0:T(2,128)S(1)} %copy.26), channel_id=1, replica_groups=mesh['grp'=8,'tp'=32] {'tp'}, dimensions={0} | all-to-all | bytes 4194304 | tf_op jit(solution)/shard_map/all_to_all | solution.py:52
  324.0 1.4 reduce_sum.69
  (19 shorter events, 0.2 us)
Async XLA Ops:
  6.5 264.1 %copy-start = (bf16[4096,64]{0,1:T(8,128)(2,1)S(1)}, bf16[4096,64]{0,1:T(8,128)(2,1)}, u32[]{:S(2)}) copy-start(bf16[4096,64]{0,1:T(8,128)(2,1)} %param.17) | copy-start | bytes 1572868
  6.5 128.4 %reduce-scatter.2.cloned.1.call-start = ((), (), s32[]{:S(2)}) async-start(), calls=%async_computation.7 | async-start | bytes 9437184 | tf_op jit(solution)/shard_map/reduce_scatter | solution.py:90
  41.9 1.0 copy-start.4
  41.9 1.0 copy-start.6
  41.9 187.5 %all-gather.4.cloned.1.call-start = ((), (), s32[]{:S(2)}) async-start(), calls=%async_computation.8 | async-start | bytes 9437184 | tf_op jit(solution)/shard_map/all_gather | solution.py:108
  42.9 3.9 %copy-start.1 = (bf16[512,4008]{0,1:T(8,128)(2,1)S(1)}, bf16[512,4008]{0,1:T(8,128)(2,1)}, u32[]{:S(2)}) copy-start(bf16[512,4008]{0,1:T(8,128)(2,1)} %param.13) | copy-start | bytes 12312580
  46.7 2.5 copy-start.10
  46.7 2.6 copy-start.7
  46.7 2.6 copy-start.8
  136.9 14.5 %all-to-all-start.1 = ((f32[32,1,64]{2,1,0:T(1,128)}), f32[32,1,64]{2,1,0:T(1,128)S(1)}, u32[]{:S(2)}, u32[]{:S(2)}) async-start(f32[32,1,64]{2,1,0:T(1,128)} %broadcast_in_dim.38), calls=%async_computation.2 | async-start | bytes 32768 | tf_op jit(solution)/shard_map/all_to_all | solution.py:12
  153.6 80.8 %all-to-all-start.2 = ((f32[32,1,64]{2,1,0:T(1,128)}), f32[32,1,64]{2,1,0:T(1,128)S(1)}, u32[]{:S(2)}, u32[]{:S(2)}) async-start(f32[32,1,64]{2,1,0:T(1,128)} %broadcast_in_dim.39), calls=%async_computation.3 | async-start | bytes 32768 | tf_op jit(solution)/shard_map/all_to_all | solution.py:12
  157.8 76.6 %copy-start.2 = (f32[64,4008]{1,0:T(8,128)S(1)}, f32[64,4008]{1,0:T(8,128)}, u32[]{:S(2)}) copy-start(f32[64,4008]{1,0:T(8,128)} %reduce-scatter.2.cloned.1.call-done) | copy-start | bytes 3078148
  157.8 76.6 %copy-start.9 = (s32[64]{0:T(128)S(1)}, s32[64]{0:T(128)}, u32[]{:S(2)}) copy-start(s32[64]{0:T(128)} %param.15) | copy-start | bytes 772
  157.8 77.1 %copy-start.5 = (bf16[4008,64]{0,1:T(8,128)(2,1)S(1)}, bf16[4008,64]{0,1:T(8,128)(2,1)}, u32[]{:S(2)}) copy-start(bf16[4008,64]{0,1:T(8,128)(2,1)} %param.18) | copy-start | bytes 1539076
  237.2 34.3 %copy-start.3 = (bf16[64,4096]{1,0:T(8,128)(2,1)S(1)}, bf16[64,4096]{1,0:T(8,128)(2,1)}, u32[]{:S(2)}) copy-start(bf16[64,4096]{1,0:T(8,128)(2,1)} %param.11) | copy-start | bytes 1572868
  239.3 30.2 %all-to-all-start.3 = ((f32[32,1,12352]{2,1,0:T(1,128)}), f32[32,1,12352]{2,1,0:T(1,128)S(1)}, u32[]{:S(2)}, u32[]{:S(2)}) async-start(f32[32,1,12352]{2,1,0:T(1,128)} %broadcast_in_dim.41), calls=%async_computation.4 | async-start | bytes 3178496 | tf_op jit(solution)/shard_map/all_to_all | solution.py:12
Sparse Core Ops, SparseCore 0:
  42.0 92.8 reduce-scatter.1
  136.7 92.5 all-gather.3
